TPU v7x, 256 devices: a whole 4x4x8 slice. The times are simulated.
256 devices in a mesh: tile: 64 (over z, y_lo, x), chan: 4 (over y_hi, core).
Axes of the slice: x: 4, y: 4 (y_hi: 2, y_lo: 2; y = y_hi * 2 + y_lo), z: 8, core: 2. Of those that a mesh axis runs over, the one named last changes fastest.
Arguments:
- latent: bfloat16 [2, 16, 14400], P(None, 'chan', 'tile'), may hold values from -6 to 6
- latent_cache: bfloat16 [2, 16, 14400], P(None, 'chan', 'tile'), may hold values from -6 to 6
- weight_in: bfloat16 [3, 3, 3, 384, 16], P(None, None, None, 'chan'), may hold values from -0.3125 to 0.3125
- bias_in: float32 [384], P('chan'), may hold values from -3 to 3
- cache_a: bfloat16 [2, 384, 14400], P(None, 'chan', 'tile'), may hold values from -6 to 6
- gain_a: float32 [384], P('chan'), may hold values from 0.1 to 1.9
- weight_a: bfloat16 [3, 3, 3, 384, 384], P(None, None, None, 'chan'), may hold values from -0.0625 to 0.0625
- bias_a: float32 [384], P('chan'), may hold values from -3 to 3
- cache_b: bfloat16 [2, 384, 14400], P(None, 'chan', 'tile'), may hold values from -6 to 6
- gain_b: float32 [384], P('chan'), may hold values from 0.1 to 1.9
- weight_b: bfloat16 [3, 3, 3, 384, 384], P(None, None, None, 'chan'), may hold values from -0.0625 to 0.0625
- bias_b: float32 [384], P('chan'), may hold values from -3 to 3
- weight_up: bfloat16 [3, 3, 192, 384], P(None, None, 'chan'), may hold values from -0.109375 to 0.109375
- bias_up: float32 [192], P('chan'), may hold values from -3 to 3
Outputs:
- upsampled: bfloat16 [2, 192, 57600], P(None, 'chan', 'tile')
All inputs are finite; a program needn't handle non-finite values.
Results may differ from a plain program's by a relative error of at most 0.011.
Values may be sent and summed in bfloat16 or wider, within the bound.
A program may use at most 64 MiB of HBM per device.

v0:
```python
from functools import partial
import jax
import jax.numpy as jnp
from jax import lax
from jax.sharding import PartitionSpec as P

C = 384
W = 160
eps_norm = 1e-06


def extended(block, sides, width):
    for axis, dim in sides:
        count = lax.axis_size(axis)
        forward = [(i, i + 1) for i in range(count - 1)]
        backward = [(target, source) for source, target in forward]
        low = lax.ppermute(
            lax.slice_in_dim(block, block.shape[dim] - width, None, axis=dim), axis, forward
        )
        high = lax.ppermute(lax.slice_in_dim(block, 0, width, axis=dim), axis, backward)
        block = jnp.concatenate([low, block, high], axis=dim)
    return block


def column_mask(part, column_tap, position):
    if column_tap == 0:
        return jnp.where(position > 0, part, 0.0)
    if column_tap == 2:
        return jnp.where(position < W - 1, part, 0.0)
    return part


def causal_terms(source, weight_rows, start):
    frames = source.shape[0] - 2
    count = source.shape[2] - 2 * W - 2
    position = (start + lax.iota(jnp.int32, count)) % W
    outputs = weight_rows.shape[3]
    summed = jnp.zeros((frames, outputs, count), jnp.float32)
    for column_tap in range(3):
        part = jnp.zeros((frames, outputs, count), jnp.float32)
        for time_tap in range(3):
            for row_tap in range(3):
                begin = row_tap * W + column_tap
                window = source[time_tap : time_tap + frames, :, begin : begin + count]
                part = part + jnp.einsum(
                    "ok,fkr->for",
                    weight_rows[time_tap, row_tap, column_tap],
                    window,
                    preferred_element_type=jnp.float32,
                )
        summed = summed + column_mask(part, column_tap, position)
    return summed


def upsample_terms(source, weight_rows, start):
    frames = source.shape[0]
    count = source.shape[2] - 2 * W - 2
    position = (start + lax.iota(jnp.int32, count)) % W
    outputs = weight_rows.shape[2]
    quarters = []
    for row_half in range(2):
        for column_half in range(2):
            summed = jnp.zeros((frames, outputs, count), jnp.float32)
            for column_step in range(3):
                part = jnp.zeros((frames, outputs, count), jnp.float32)
                for row_tap in range(3):
                    row_step = (row_half + row_tap - 1) // 2
                    for column_tap in range(3):
                        if (column_half + column_tap - 1) // 2 != column_step - 1:
                            continue
                        begin = (row_step + 1) * W + column_step
                        window = source[:, :, begin : begin + count]
                        part = part + jnp.einsum(
                            "ok,fkr->for",
                            weight_rows[row_tap, column_tap],
                            window,
                            preferred_element_type=jnp.float32,
                        )
                summed = summed + column_mask(part, column_step, position)
            quarters.append(summed)
    stacked = jnp.stack(quarters, -1)
    return stacked.reshape(frames, outputs, 4 * count)


def convolve(source, weight, kernel_fn):
    complete = lax.all_gather(source, "chan", axis=1, tiled=True)
    rimmed = extended(complete, (("tile", 2),), W + 1)
    return kernel_fn(rimmed, weight)


def activate(features, gain_vector):
    values = features.astype(jnp.float32)
    squares = jnp.sum(values * values, axis=1)
    total_sq = lax.psum(squares, "chan")
    inverse_rms = lax.rsqrt(total_sq / C + eps_norm)
    return jax.nn.silu(values * inverse_rms[:, None, :] * gain_vector[None, :, None]).astype(
        jnp.bfloat16
    )


def shards(
    latent,
    latent_cache,
    weight_in,
    bias_in,
    cache_a,
    gain_a,
    weight_a,
    bias_a,
    cache_b,
    gain_b,
    weight_b,
    bias_b,
    weight_up,
    bias_up,
):
    span = latent.shape[2]
    start = lax.axis_index("tile") * span
    causal_fn = partial(causal_terms, start=start)
    upsample_fn = partial(upsample_terms, start=start)
    stem_sum = convolve(jnp.concatenate([latent_cache, latent], 0), weight_in, causal_fn)
    stem_out = (stem_sum + bias_in[None, :, None]).astype(jnp.bfloat16)
    active_a = activate(stem_out, gain_a)
    inner_sum = convolve(jnp.concatenate([cache_a, active_a], 0), weight_a, causal_fn)
    inner_out = (inner_sum + bias_a[None, :, None]).astype(jnp.bfloat16)
    active_b = activate(inner_out, gain_b)
    branch_sum = convolve(jnp.concatenate([cache_b, active_b], 0), weight_b, causal_fn)
    residual_out = (stem_out.astype(jnp.float32) + branch_sum + bias_b[None, :, None]).astype(
        jnp.bfloat16
    )
    upsample_sum = convolve(residual_out, weight_up, upsample_fn)
    return (upsample_sum + bias_up[None, :, None]).astype(jnp.bfloat16)


def solution(mesh):
    placed = (
        P(None, "chan", "tile"),
        P(None, "chan", "tile"),
        P(None, None, None, "chan", None),
        P("chan"),
        P(None, "chan", "tile"),
        P("chan"),
        P(None, None, None, "chan", None),
        P("chan"),
        P(None, "chan", "tile"),
        P("chan"),
        P(None, None, None, "chan", None),
        P("chan"),
        P(None, None, "chan", None),
        P("chan"),
    )
    return jax.shard_map(
        shards, mesh=mesh, in_specs=placed, out_specs=P(None, "chan", "tile"), check_vma=False
    )
```

profile of v0, /device:TPU:128, one launch (start us, length us, event | category | flops | bytes accessed | tf_op | source)
XLA Modules:
  0.0 182.4 jit_solution(865237823081435494)
XLA Ops:
  1.4 6.7 %all_gather.12 = bf16[4,16,225]{2,0,1:T(4,128)(2,1)S(1)} all-gather(bf16[4,4,225]{2,0,1:T(4,128)(2,1)S(1)} %pad_maximum_fusion.19), channel_id=1, replica_groups=mesh['tile'=64,'chan'=4] {'chan'}, dimensions={1}, use_global_device_ids=true | all-gather | bytes 36000 | tf_op jit(solution)/shard_map/all_gather | solution.py:86
  8.2 5.2 %collective-permute-start.1 = (bf16[4,16,161]{2,1,0:T(8,128)(2,1)S(1)}, bf16[4,16,161]{2,1,0:T(8,128)(2,1)S(1)}, u32[]{:S(2)}, u32[]{:S(2)}) collective-permute-start(bf16[4,16,161]{2,1,0:T(8,128)(2,1)S(1)} %get-tuple-element.18), channel_id=1, source_target_pairs={{4,0},{8,4},{12,8},{16,12},{20,16},{24,20},{28,24},{32,28},{36,32}... | collective-permute-start | bytes 61832 | tf_op jit(solution)/shard_map/ppermute | solution.py:20
  13.4 1.9 %collective-permute-start = (bf16[4,16,161]{2,1,0:T(8,128)(2,1)S(1)}, bf16[4,16,161]{2,1,0:T(8,128)(2,1)S(1)}, u32[]{:S(2)}, u32[]{:S(2)}) collective-permute-start(bf16[4,16,161]{2,1,0:T(8,128)(2,1)S(1)} %get-tuple-element.17), channel_id=1, source_target_pairs={{0,4},{4,8},{8,12},{12,16},{16,20},{20,24},{24,28},{28,32},{32,36}... | collective-permute-start | bytes 61832 | tf_op jit(solution)/shard_map/ppermute | solution.py:17
  18.1 0.9 fusion.494
  19.0 0.9 fusion.434
  20.0 0.9 fusion.462
  20.9 0.9 fusion.459
  21.8 1.6 collective-permute-done
  28.5 8.6 %psum.14 = f32[2,225]{1,0:T(2,128)S(1)} all-reduce(f32[2,225]{1,0:T(2,128)S(1)} %get-tuple-element.19), channel_id=1, replica_groups=mesh['tile'=64,'chan'=4] {'chan'}, use_global_device_ids=true, to_apply=%region_1.2 | all-reduce | flops 450 | bytes 3600 | tf_op jit(solution)/shard_map/psum | solution.py:94
  37.3 8.9 %all_gather.13 = bf16[4,384,225]{2,1,0:T(8,128)(2,1)S(1)} all-gather(bf16[4,96,225]{2,1,0:T(8,128)(2,1)S(1)} %pad_maximum_fusion.13), channel_id=1, replica_groups=mesh['tile'=64,'chan'=4] {'chan'}, dimensions={1}, use_global_device_ids=true | all-gather | bytes 864000 | tf_op jit(solution)/shard_map/all_gather | solution.py:86
  47.4 6.6 %collective-permute-start.3 = (bf16[4,384,161]{1,0,2:T(4,128)(2,1)S(1)}, bf16[4,384,161]{1,0,2:T(4,128)(2,1)}, u32[]{:S(2)}, u32[]{:S(2)}) collective-permute-start(bf16[4,384,161]{1,0,2:T(4,128)(2,1)S(1)} %copy.259), channel_id=1, source_target_pairs={{4,0},{8,4},{12,8},{16,12},{20,16},{24,20},{28,24},{32,28},{36,32}... | collective-permute-start | bytes 1483784 | tf_op jit(solution)/shard_map/ppermute | solution.py:20
  54.9 1.9 %collective-permute-start.2 = (bf16[4,384,161]{1,0,2:T(4,128)(2,1)S(1)}, bf16[4,384,161]{1,0,2:T(4,128)(2,1)}, u32[]{:S(2)}, u32[]{:S(2)}) collective-permute-start(bf16[4,384,161]{1,0,2:T(4,128)(2,1)S(1)} %copy.255), channel_id=1, source_target_pairs={{0,4},{4,8},{8,12},{12,16},{16,20},{20,24},{24,28},{28,32},{32,36}... | collective-permute-start | bytes 1483784 | tf_op jit(solution)/shard_map/ppermute | solution.py:17
  56.8 1.1 fusion.297
  57.9 1.8 fusion.301
  59.7 1.8 fusion.305
  61.5 3.6 %collective-permute-done.3 = bf16[4,384,161]{1,0,2:T(4,128)(2,1)} collective-permute-done((bf16[4,384,161]{1,0,2:T(4,128)(2,1)S(1)}, bf16[4,384,161]{1,0,2:T(4,128)(2,1)}, u32[]{:S(2)}, u32[]{:S(2)}) %collective-permute-start.3) | collective-permute-done | bytes 494624 | tf_op jit(solution)/shard_map/ppermute | solution.py:20
  65.0 1.6 copy.260
  66.6 1.3 fusion.175
  67.9 1.3 fusion.213
  69.2 1.3 fusion.197
  70.5 1.3 fusion.199
  71.7 2.6 %collective-permute-done.2 = bf16[4,384,161]{1,0,2:T(4,128)(2,1)} collective-permute-done((bf16[4,384,161]{1,0,2:T(4,128)(2,1)S(1)}, bf16[4,384,161]{1,0,2:T(4,128)(2,1)}, u32[]{:S(2)}, u32[]{:S(2)}) %collective-permute-start.2) | collective-permute-done | bytes 494624 | tf_op jit(solution)/shard_map/ppermute | solution.py:17
  74.3 1.6 copy.256
  75.9 1.4 fusion.177
  77.3 1.3 fusion.195
  86.1 8.7 %psum.15 = f32[2,225]{1,0:T(2,128)S(1)} all-reduce(f32[2,225]{1,0:T(2,128)S(1)} %get-tuple-element.21), channel_id=1, replica_groups=mesh['tile'=64,'chan'=4] {'chan'}, use_global_device_ids=true, to_apply=%region_3.4 | all-reduce | flops 450 | bytes 3600 | tf_op jit(solution)/shard_map/psum | solution.py:94
  95.0 8.7 %all_gather.14 = bf16[4,384,225]{2,1,0:T(8,128)(2,1)S(1)} all-gather(bf16[4,96,225]{2,1,0:T(8,128)(2,1)S(1)} %pad_maximum_fusion.14), channel_id=1, replica_groups=mesh['tile'=64,'chan'=4] {'chan'}, dimensions={1}, use_global_device_ids=true | all-gather | bytes 864000 | tf_op jit(solution)/shard_map/all_gather | solution.py:86
  104.9 5.8 %collective-permute-start.5 = (bf16[4,384,161]{1,0,2:T(4,128)(2,1)S(1)}, bf16[4,384,161]{1,0,2:T(4,128)(2,1)}, u32[]{:S(2)}, u32[]{:S(2)}) collective-permute-start(bf16[4,384,161]{1,0,2:T(4,128)(2,1)S(1)} %copy.290), channel_id=1, source_target_pairs={{4,0},{8,4},{12,8},{16,12},{20,16},{24,20},{28,24},{32,28},{36,32}... | collective-permute-start | bytes 1483784 | tf_op jit(solution)/shard_map/ppermute | solution.py:20
  111.6 1.9 %collective-permute-start.4 = (bf16[4,384,161]{1,0,2:T(4,128)(2,1)S(1)}, bf16[4,384,161]{1,0,2:T(4,128)(2,1)}, u32[]{:S(2)}, u32[]{:S(2)}) collective-permute-start(bf16[4,384,161]{1,0,2:T(4,128)(2,1)S(1)} %copy.286), channel_id=1, source_target_pairs={{0,4},{4,8},{8,12},{12,16},{16,20},{20,24},{24,28},{28,32},{32,36}... | collective-permute-start | bytes 1483784 | tf_op jit(solution)/shard_map/ppermute | solution.py:17
  113.6 1.1 fusion.267
  114.7 1.8 fusion.271
  116.4 1.8 fusion.275
  118.2 3.6 %collective-permute-done.5 = bf16[4,384,161]{1,0,2:T(4,128)(2,1)} collective-permute-done((bf16[4,384,161]{1,0,2:T(4,128)(2,1)S(1)}, bf16[4,384,161]{1,0,2:T(4,128)(2,1)}, u32[]{:S(2)}, u32[]{:S(2)}) %collective-permute-start.5) | collective-permute-done | bytes 494624 | tf_op jit(solution)/shard_map/ppermute | solution.py:20
  121.8 1.6 copy.291
  123.4 1.3 fusion.171
  124.7 1.3 fusion.247
  126.0 1.3 fusion.231
  127.2 1.3 fusion.233
  128.5 2.6 %collective-permute-done.4 = bf16[4,384,161]{1,0,2:T(4,128)(2,1)} collective-permute-done((bf16[4,384,161]{1,0,2:T(4,128)(2,1)S(1)}, bf16[4,384,161]{1,0,2:T(4,128)(2,1)}, u32[]{:S(2)}, u32[]{:S(2)}) %collective-permute-start.4) | collective-permute-done | bytes 494624 | tf_op jit(solution)/shard_map/ppermute | solution.py:17
  131.1 1.6 copy.287
  132.7 1.4 fusion.173
  134.1 1.3 fusion.229
  142.9 7.7 %all_gather.15 = bf16[2,384,225]{2,1,0:T(8,128)(2,1)S(1)} all-gather(bf16[2,96,225]{2,1,0:T(8,128)(2,1)S(1)} %fusion.76), channel_id=1, replica_groups=mesh['tile'=64,'chan'=4] {'chan'}, dimensions={1}, use_global_device_ids=true | all-gather | bytes 432000 | tf_op jit(solution)/shard_map/all_gather | solution.py:86
  151.5 6.1 %collective-permute-start.7 = (bf16[2,384,161]{2,1,0:T(8,128)(2,1)S(1)}, bf16[2,384,161]{2,1,0:T(8,128)(2,1)S(1)}, u32[]{:S(2)}, u32[]{:S(2)}) collective-permute-start(bf16[2,384,161]{2,1,0:T(8,128)(2,1)S(1)} %get-tuple-element.16), channel_id=1, source_target_pairs={{4,0},{8,4},{12,8},{16,12},{20,16},{24,20},{28,24},{32,28},{36,32}... | collective-permute-start | bytes 741896 | tf_op jit(solution)/shard_map/ppermute | solution.py:20
  157.6 2.1 %collective-permute-start.6 = (bf16[2,384,161]{2,1,0:T(8,128)(2,1)S(1)}, bf16[2,384,161]{2,1,0:T(8,128)(2,1)S(1)}, u32[]{:S(2)}, u32[]{:S(2)}) collective-permute-start(bf16[2,384,161]{2,1,0:T(8,128)(2,1)S(1)} %get-tuple-element.15), channel_id=1, source_target_pairs={{0,4},{4,8},{8,12},{12,16},{16,20},{20,24},{24,28},{28,32},{32,36}... | collective-permute-start | bytes 741896 | tf_op jit(solution)/shard_map/ppermute | solution.py:17
  160.1 6.3 %collective-permute-done.7 = bf16[2,384,161]{2,1,0:T(8,128)(2,1)S(1)} collective-permute-done((bf16[2,384,161]{2,1,0:T(8,128)(2,1)S(1)}, bf16[2,384,161]{2,1,0:T(8,128)(2,1)S(1)}, u32[]{:S(2)}, u32[]{:S(2)}) %collective-permute-start.7) | collective-permute-done | bytes 247328 | tf_op jit(solution)/shard_map/ppermute | solution.py:20
  166.5 8.3 %collective-permute-done.6 = bf16[2,384,161]{2,1,0:T(8,128)(2,1)S(1)} collective-permute-done((bf16[2,384,161]{2,1,0:T(8,128)(2,1)S(1)}, bf16[2,384,161]{2,1,0:T(8,128)(2,1)S(1)}, u32[]{:S(2)}, u32[]{:S(2)}) %collective-permute-start.6) | collective-permute-done | bytes 247328 | tf_op jit(solution)/shard_map/ppermute | solution.py:17
  174.8 1.0 fusion.110
  (140 shorter events, 36.0 us)
Async XLA Ops:
  0.0 23.5 %copy-start.7 = (bf16[3,3,3,96,16]{3,4,2,1,0:T(8,128)(2,1)S(1)}, bf16[3,3,3,96,16]{3,4,2,1,0:T(8,128)(2,1)}, u32[]{:S(2)}) copy-start(bf16[3,3,3,96,16]{3,4,2,1,0:T(8,128)(2,1)} %param.16) | copy-start | bytes 248836
  8.2 9.9 %collective-permute-start.1 = (bf16[4,16,161]{2,1,0:T(8,128)(2,1)S(1)}, bf16[4,16,161]{2,1,0:T(8,128)(2,1)S(1)}, u32[]{:S(2)}, u32[]{:S(2)}) collective-permute-start(bf16[4,16,161]{2,1,0:T(8,128)(2,1)S(1)} %get-tuple-element.18), channel_id=1, source_target_pairs={{4,0},{8,4},{12,8},{16,12},{20,16},{24,20},{28,24},{32,28},{36,32}... | collective-permute-start | bytes 61832 | tf_op jit(solution)/shard_map/ppermute | solution.py:20
  13.4 10.0 %collective-permute-start = (bf16[4,16,161]{2,1,0:T(8,128)(2,1)S(1)}, bf16[4,16,161]{2,1,0:T(8,128)(2,1)S(1)}, u32[]{:S(2)}, u32[]{:S(2)}) collective-permute-start(bf16[4,16,161]{2,1,0:T(8,128)(2,1)S(1)} %get-tuple-element.17), channel_id=1, source_target_pairs={{0,4},{4,8},{8,12},{12,16},{16,20},{20,24},{24,28},{28,32},{32,36}... | collective-permute-start | bytes 61832 | tf_op jit(solution)/shard_map/ppermute | solution.py:17
  27.6 0.7 copy-start.10
  27.6 9.5 %copy-start.11 = (f32[96]{0:T(128)S(1)}, f32[96]{0:T(128)}, u32[]{:S(2)}) copy-start(f32[96]{0:T(128)} %param.19) | copy-start | bytes 1156
  27.6 9.6 %copy-start.8 = (bf16[2,96,225]{2,1,0:T(8,128)(2,1)S(1)}, bf16[2,96,225]{2,1,0:T(8,128)(2,1)}, u32[]{:S(2)}) copy-start(bf16[2,96,225]{2,1,0:T(8,128)(2,1)} %param.18) | copy-start | bytes 259204
  47.4 17.6 %collective-permute-start.3 = (bf16[4,384,161]{1,0,2:T(4,128)(2,1)S(1)}, bf16[4,384,161]{1,0,2:T(4,128)(2,1)}, u32[]{:S(2)}, u32[]{:S(2)}) collective-permute-start(bf16[4,384,161]{1,0,2:T(4,128)(2,1)S(1)} %copy.259), channel_id=1, source_target_pairs={{4,0},{8,4},{12,8},{16,12},{20,16},{24,20},{28,24},{32,28},{36,32}... | collective-permute-start | bytes 1483784 | tf_op jit(solution)/shard_map/ppermute | solution.py:20
  54.9 19.5 %collective-permute-start.2 = (bf16[4,384,161]{1,0,2:T(4,128)(2,1)S(1)}, bf16[4,384,161]{1,0,2:T(4,128)(2,1)}, u32[]{:S(2)}, u32[]{:S(2)}) collective-permute-start(bf16[4,384,161]{1,0,2:T(4,128)(2,1)S(1)} %copy.255), channel_id=1, source_target_pairs={{0,4},{4,8},{8,12},{12,16},{16,20},{20,24},{24,28},{28,32},{32,36}... | collective-permute-start | bytes 1483784 | tf_op jit(solution)/shard_map/ppermute | solution.py:17
  75.9 2.7 %copy-start.1 = (bf16[3,3,3,96,384]{4,3,2,1,0:T(8,128)(2,1)S(1)}, bf16[3,3,3,96,384]{4,3,2,1,0:T(8,128)(2,1)}, u32[]{:S(2)}) copy-start(bf16[3,3,3,96,384]{4,3,2,1,0:T(8,128)(2,1)} %param.20) | copy-start | bytes 5971972
  82.7 0.9 copy-start.3
  82.7 1.0 copy-start.4
  85.0 0.7 copy-start.12
  85.7 9.1 %copy-start.13 = (f32[96]{0:T(128)S(1)}, f32[96]{0:T(128)}, u32[]{:S(2)}) copy-start(f32[96]{0:T(128)} %param.23) | copy-start | bytes 1156
  85.7 9.3 %copy-start.9 = (bf16[2,96,225]{2,1,0:T(8,128)(2,1)S(1)}, bf16[2,96,225]{2,1,0:T(8,128)(2,1)}, u32[]{:S(2)}) copy-start(bf16[2,96,225]{2,1,0:T(8,128)(2,1)} %param.22) | copy-start | bytes 259204
  104.9 16.9 %collective-permute-start.5 = (bf16[4,384,161]{1,0,2:T(4,128)(2,1)S(1)}, bf16[4,384,161]{1,0,2:T(4,128)(2,1)}, u32[]{:S(2)}, u32[]{:S(2)}) collective-permute-start(bf16[4,384,161]{1,0,2:T(4,128)(2,1)S(1)} %copy.290), channel_id=1, source_target_pairs={{4,0},{8,4},{12,8},{16,12},{20,16},{24,20},{28,24},{32,28},{36,32}... | collective-permute-start | bytes 1483784 | tf_op jit(solution)/shard_map/ppermute | solution.py:20
  111.6 19.5 %collective-permute-start.4 = (bf16[4,384,161]{1,0,2:T(4,128)(2,1)S(1)}, bf16[4,384,161]{1,0,2:T(4,128)(2,1)}, u32[]{:S(2)}, u32[]{:S(2)}) collective-permute-start(bf16[4,384,161]{1,0,2:T(4,128)(2,1)S(1)} %copy.286), channel_id=1, source_target_pairs={{0,4},{4,8},{8,12},{12,16},{16,20},{20,24},{24,28},{28,32},{32,36}... | collective-permute-start | bytes 1483784 | tf_op jit(solution)/shard_map/ppermute | solution.py:17
  132.7 2.7 %copy-start.2 = (bf16[3,3,3,96,384]{4,3,2,1,0:T(8,128)(2,1)S(1)}, bf16[3,3,3,96,384]{4,3,2,1,0:T(8,128)(2,1)}, u32[]{:S(2)}) copy-start(bf16[3,3,3,96,384]{4,3,2,1,0:T(8,128)(2,1)} %param.24) | copy-start | bytes 5971972
  139.5 0.9 copy-start.5
  139.5 1.0 copy-start.6
  141.8 0.7 copy-start.15
  142.4 8.3 %copy-start = (bf16[3,3,48,384]{3,2,1,0:T(8,128)(2,1)S(1)}, bf16[3,3,48,384]{3,2,1,0:T(8,128)(2,1)}, u32[]{:S(2)}) copy-start(bf16[3,3,48,384]{3,2,1,0:T(8,128)(2,1)} %param.26) | copy-start | bytes 995332
  151.5 15.0 %collective-permute-start.7 = (bf16[2,384,161]{2,1,0:T(8,128)(2,1)S(1)}, bf16[2,384,161]{2,1,0:T(8,128)(2,1)S(1)}, u32[]{:S(2)}, u32[]{:S(2)}) collective-permute-start(bf16[2,384,161]{2,1,0:T(8,128)(2,1)S(1)} %get-tuple-element.16), channel_id=1, source_target_pairs={{4,0},{8,4},{12,8},{16,12},{20,16},{24,20},{28,24},{32,28},{36,32}... | collective-permute-start | bytes 741896 | tf_op jit(solution)/shard_map/ppermute | solution.py:20
  157.6 17.2 %collective-permute-start.6 = (bf16[2,384,161]{2,1,0:T(8,128)(2,1)S(1)}, bf16[2,384,161]{2,1,0:T(8,128)(2,1)S(1)}, u32[]{:S(2)}, u32[]{:S(2)}) collective-permute-start(bf16[2,384,161]{2,1,0:T(8,128)(2,1)S(1)} %get-tuple-element.15), channel_id=1, source_target_pairs={{0,4},{4,8},{8,12},{12,16},{16,20},{20,24},{24,28},{28,32},{32,36}... | collective-permute-start | bytes 741896 | tf_op jit(solution)/shard_map/ppermute | solution.py:17
  180.1 1.6 copy-start.14
where the time goes:
time: 184 us; the launch traced here: 182 us
  matrix products  54.8 us (30%)
  blocking collectives  49.3 us (27%)
  starting transfers between devices  31.7 us (17%)
  waiting for transfers between devices  28.7 us (16%)
  local copies, waits for them, and re-layouts  14.8 us (8%)
  other arithmetic  2.17 us (1%)
    dot_general x81, matrix products, causal_terms(): jnp.einsum('ok,fkr->for', weight_rows[time_tap, row_tap, column_tap], win...  49.7 us
    all_gather x4, blocking collectives, convolve(): complete = lax.all_gather(source, 'chan', axis=1, tiled=True)  32 us
    ppermute x4, starting transfers between devices, extended(): lax.ppermute(lax.slice_in_dim(block, 0, width, axis=dim), axis, backward)  23.8 us
    psum x2, blocking collectives, activate(): total_sq = lax.psum(squares, 'chan')  17.2 us
    ppermute x4, waiting for transfers between devices, extended(): lax.ppermute(lax.slice_in_dim(block, block.shape[dim] - width, None, axis...  15.2 us
    ppermute x4, waiting for transfers between devices, extended(): lax.ppermute(lax.slice_in_dim(block, 0, width, axis=dim), axis, backward)  13.5 us
    ppermute x4, starting transfers between devices, extended(): lax.ppermute(lax.slice_in_dim(block, block.shape[dim] - width, None, axis...  7.9 us
    dot_general x25, matrix products, upsample_terms(): jnp.einsum('ok,fkr->for', weight_rows[row_tap, column_tap], window, prefe...  5.11 us
  transfers between devices with their start and end apart: 8, of which 7 were waited for; matrix products, arithmetic and copies ran while one was open for 17% of the time, Pallas kernels for 0%

commit v1 on v0

--- a/solution.py
+++ b/solution.py
@@ -83,7 +83,9 @@
 
 
 def convolve(source, weight, kernel_fn):
-    complete = lax.all_gather(source, "chan", axis=1, tiled=True)
+    complete = jnp.concatenate(
+        lax.all_to_all(jnp.stack([source] * lax.axis_size("chan")), "chan", 0, 0), axis=1
+    )
     rimmed = extended(complete, (("tile", 2),), W + 1)
     return kernel_fn(rimmed, weight)
 

time: 184 us -> 176 us (0.957)
  matrix products: 54.8 us -> 31.7 us
  waiting for transfers between devices: 28.7 us -> 45.3 us
  local copies, waits for them, and re-layouts: 14.8 us -> 6.49 us
  blocking collectives: 49.3 us -> 57.4 us
    all_to_all x0 -> x3, blocking collectives: none -> 42.7 us  [convolve(): lax.all_to_all(jnp.stack([source] * lax.axis_size('chan')), 'chan', 0, 0)]
    all_gather x4 -> x0, blocking collectives: 32 us -> none  [convolve(): complete = lax.all_gather(source, 'chan', axis=1, tiled=True)]
    dot_general x81, matrix products: 49.7 us -> 26 us  [causal_terms(): jnp.einsum('ok,fkr->for', weight_rows[time_tap, row_tap, column_tap], win...]
    ppermute x4, starting transfers between devices: 23.8 us -> 15 us  [extended(): lax.ppermute(lax.slice_in_dim(block, 0, width, axis=dim), axis, backward)]
    ppermute x4 -> x0, local copies, waits for them, and re-layouts: 6.3 us -> none  [the longest x2 3.15 us: extended(): lax.ppermute(lax.slice_in_dim(block, block.shape[dim] - width, None, axis...]
    ppermute x4, waiting for transfers between devices: 13.5 us -> 19.3 us  [extended(): lax.ppermute(lax.slice_in_dim(block, 0, width, axis=dim), axis, backward)]
    all_to_all x0 -> x1, waiting for transfers between devices: none -> 5.43 us  [convolve(): lax.all_to_all(jnp.stack([source] * lax.axis_size('chan')), 'chan', 0, 0)]
    ppermute x4, waiting for transfers between devices: 15.2 us -> 20.5 us  [extended(): lax.ppermute(lax.slice_in_dim(block, block.shape[dim] - width, None, axis...]
  transfers between devices with their start and end apart: 8 -> 9, of which waited for: 7 -> 8; matrix products, arithmetic and copies ran while one was open for 17% -> 6% of each run, Pallas kernels for 0% -> 0%
where the time goes in v1:
time: 176 us; the launch traced here: 175 us
  blocking collectives  57.4 us (33%)
  waiting for transfers between devices  45.3 us (26%)
  matrix products  31.7 us (18%)
  starting transfers between devices  31.3 us (18%)
  local copies, waits for them, and re-layouts  6.49 us (4%)
  other arithmetic  2.22 us (1%)
    all_to_all x3, blocking collectives, convolve(): lax.all_to_all(jnp.stack([source] * lax.axis_size('chan')), 'chan', 0, 0)  42.7 us
    dot_general x81, matrix products, causal_terms(): jnp.einsum('ok,fkr->for', weight_rows[time_tap, row_tap, column_tap], win...  26 us
    ppermute x4, waiting for transfers between devices, extended(): lax.ppermute(lax.slice_in_dim(block, block.shape[dim] - width, None, axis...  20.5 us
    ppermute x4, waiting for transfers between devices, extended(): lax.ppermute(lax.slice_in_dim(block, 0, width, axis=dim), axis, backward)  19.3 us
    ppermute x4, starting transfers between devices, extended(): lax.ppermute(lax.slice_in_dim(block, 0, width, axis=dim), axis, backward)  15 us
    psum x2, blocking collectives, activate(): total_sq = lax.psum(squares, 'chan')  14.7 us
    ppermute x4, starting transfers between devices, extended(): lax.ppermute(lax.slice_in_dim(block, block.shape[dim] - width, None, axis...  11.9 us
    dot_general x25, matrix products, upsample_terms(): jnp.einsum('ok,fkr->for', weight_rows[row_tap, column_tap], window, prefe...  5.74 us
  transfers between devices with their start and end apart: 9, of which 8 were waited for; matrix products, arithmetic and copies ran while one was open for 6% of the time, Pallas kernels for 0%

profile of v1, /device:TPU:128, one launch (start us, length us, event | category | flops | bytes accessed | tf_op | source)
XLA Modules:
  0.0 175.5 jit_solution(13320483096530738501)
XLA Ops:
  0.0 0.7 pad_maximum_fusion.19
  0.8 0.6 stack.18
  1.4 4.5 %all-to-all-start = ((bf16[4,4,4,225]{3,2,1,0:T(4,128)(2,1)}), bf16[4,4,4,225]{3,2,1,0:T(4,128)(2,1)S(1)}, u32[]{:S(2)}, u32[]{:S(2)}) async-start(bf16[4,4,4,225]{3,2,1,0:T(4,128)(2,1)} %stack.18), calls=%async_computation | async-start | bytes 65536 | tf_op jit(solution)/shard_map/all_to_all | solution.py:87
  5.9 5.4 %all-to-all-done = bf16[4,4,4,225]{3,2,1,0:T(4,128)(2,1)S(1)} async-done(((bf16[4,4,4,225]{3,2,1,0:T(4,128)(2,1)}), bf16[4,4,4,225]{3,2,1,0:T(4,128)(2,1)S(1)}, u32[]{:S(2)}, u32[]{:S(2)}) %all-to-all-start) | async-done | bytes 28832 | tf_op jit(solution)/shard_map/all_to_all | solution.py:87
  11.5 4.3 %collective-permute-start.1 = (bf16[4,16,161]{2,1,0:T(8,128)(2,1)S(1)}, bf16[4,16,161]{2,1,0:T(8,128)(2,1)S(1)}, u32[]{:S(2)}, u32[]{:S(2)}) collective-permute-start(bf16[4,16,161]{2,1,0:T(8,128)(2,1)S(1)} %get-tuple-element.27), channel_id=1, source_target_pairs={{4,0},{8,4},{12,8},{16,12},{20,16},{24,20},{28,24},{32,28},{36,32}... | collective-permute-start | bytes 61832 | tf_op jit(solution)/shard_map/ppermute | solution.py:20
  15.8 1.9 %collective-permute-start = (bf16[4,16,161]{2,1,0:T(8,128)(2,1)S(1)}, bf16[4,16,161]{2,1,0:T(8,128)(2,1)S(1)}, u32[]{:S(2)}, u32[]{:S(2)}) collective-permute-start(bf16[4,16,161]{2,1,0:T(8,128)(2,1)S(1)} %get-tuple-element.26), channel_id=1, source_target_pairs={{0,4},{4,8},{8,12},{12,16},{16,20},{20,24},{24,28},{28,32},{32,36}... | collective-permute-start | bytes 61832 | tf_op jit(solution)/shard_map/ppermute | solution.py:17
  17.8 0.9 fusion.508
  18.7 0.9 fusion.512
  19.6 0.9 fusion.516
  20.5 0.9 fusion.494
  21.5 0.9 fusion.434
  22.4 0.9 fusion.462
  23.6 2.2 %collective-permute-done = bf16[4,16,161]{2,1,0:T(8,128)(2,1)S(1)} collective-permute-done((bf16[4,16,161]{2,1,0:T(8,128)(2,1)S(1)}, bf16[4,16,161]{2,1,0:T(8,128)(2,1)S(1)}, u32[]{:S(2)}, u32[]{:S(2)}) %collective-permute-start) | collective-permute-done | bytes 20640 | tf_op jit(solution)/shard_map/ppermute | solution.py:17
  30.8 7.5 %psum.14 = f32[2,225]{1,0:T(2,128)S(1)} all-reduce(f32[2,225]{1,0:T(2,128)S(1)} %get-tuple-element.28), channel_id=1, replica_groups=mesh['tile'=64,'chan'=4] {'chan'}, use_global_device_ids=true, to_apply=%region_1.2 | all-reduce | flops 450 | bytes 3600 | tf_op jit(solution)/shard_map/psum | solution.py:96
  38.6 15.6 %all_to_all.20 = bf16[4,4,96,225]{3,2,1,0:T(8,128)(2,1)S(1)} all-to-all(bf16[4,4,96,225]{3,2,1,0:T(8,128)(2,1)S(1)} %stack.19), channel_id=1, replica_groups=mesh['tile'=64,'chan'=4] {'chan'}, dimensions={0} | all-to-all | bytes 1382400 | tf_op jit(solution)/shard_map/all_to_all | solution.py:87
  54.2 1.1 fusion.632
  55.3 0.3 copy.94
  55.8 6.7 %collective-permute-start.3 = (bf16[4,384,161]{1,2,0:T(8,128)(2,1)S(1)}, bf16[4,384,161]{1,2,0:T(8,128)(2,1)S(1)}, u32[]{:S(2)}, u32[]{:S(2)}) collective-permute-start(bf16[4,384,161]{1,2,0:T(8,128)(2,1)S(1)} %get-tuple-element.14), channel_id=1, source_target_pairs={{4,0},{8,4},{12,8},{16,12},{20,16},{24,20},{28,24},{32,28},{36,32}... | collective-permute-start | bytes 1483784 | tf_op jit(solution)/shard_map/ppermute | solution.py:20
  62.5 1.9 %collective-permute-start.2 = (bf16[4,384,161]{1,2,0:T(8,128)(2,1)S(1)}, bf16[4,384,161]{1,2,0:T(8,128)(2,1)S(1)}, u32[]{:S(2)}, u32[]{:S(2)}) collective-permute-start(bf16[4,384,161]{1,2,0:T(8,128)(2,1)S(1)} %get-tuple-element.13), channel_id=1, source_target_pairs={{0,4},{4,8},{8,12},{12,16},{16,20},{20,24},{24,28},{28,32},{32,36}... | collective-permute-start | bytes 1483784 | tf_op jit(solution)/shard_map/ppermute | solution.py:17
  65.2 7.9 %collective-permute-done.3 = bf16[4,384,161]{1,2,0:T(8,128)(2,1)S(1)} collective-permute-done((bf16[4,384,161]{1,2,0:T(8,128)(2,1)S(1)}, bf16[4,384,161]{1,2,0:T(8,128)(2,1)S(1)}, u32[]{:S(2)}, u32[]{:S(2)}) %collective-permute-start.3) | collective-permute-done | bytes 494624 | tf_op jit(solution)/shard_map/ppermute | solution.py:20
  74.3 7.2 %collective-permute-done.2 = bf16[4,384,161]{1,2,0:T(8,128)(2,1)S(1)} collective-permute-done((bf16[4,384,161]{1,2,0:T(8,128)(2,1)S(1)}, bf16[4,384,161]{1,2,0:T(8,128)(2,1)S(1)}, u32[]{:S(2)}, u32[]{:S(2)}) %collective-permute-start.2) | collective-permute-done | bytes 494624 | tf_op jit(solution)/shard_map/ppermute | solution.py:17
  83.5 0.3 fusion.207
  84.4 0.3 fusion.209
  85.2 0.3 fusion.211
  86.7 0.4 fusion.65
  87.1 0.4 multiply_reduce_fusion
  87.5 7.2 %psum.15 = f32[2,225]{1,0:T(2,128)S(1)} all-reduce(f32[2,225]{1,0:T(2,128)S(1)} %get-tuple-element.30), channel_id=1, replica_groups=mesh['tile'=64,'chan'=4] {'chan'}, use_global_device_ids=true, to_apply=%region_3.4 | all-reduce | flops 450 | bytes 3600 | tf_op jit(solution)/shard_map/psum | solution.py:96
  95.0 15.7 %all_to_all.21 = bf16[4,4,96,225]{3,2,1,0:T(8,128)(2,1)S(1)} all-to-all(bf16[4,4,96,225]{3,2,1,0:T(8,128)(2,1)S(1)} %stack.20), channel_id=1, replica_groups=mesh['tile'=64,'chan'=4] {'chan'}, dimensions={0} | all-to-all | bytes 1382400 | tf_op jit(solution)/shard_map/all_to_all | solution.py:87
  110.7 1.1 fusion.631
  111.8 0.3 copy.105
  112.2 2.1 %collective-permute-start.5 = (bf16[4,384,161]{1,2,0:T(8,128)(2,1)S(1)}, bf16[4,384,161]{1,2,0:T(8,128)(2,1)S(1)}, u32[]{:S(2)}, u32[]{:S(2)}) collective-permute-start(bf16[4,384,161]{1,2,0:T(8,128)(2,1)S(1)} %get-tuple-element.12), channel_id=1, source_target_pairs={{4,0},{8,4},{12,8},{16,12},{20,16},{24,20},{28,24},{32,28},{36,32}... | collective-permute-start | bytes 1483784 | tf_op jit(solution)/shard_map/ppermute | solution.py:20
  114.3 4.1 %collective-permute-start.4 = (bf16[4,384,161]{1,2,0:T(8,128)(2,1)S(1)}, bf16[4,384,161]{1,2,0:T(8,128)(2,1)S(1)}, u32[]{:S(2)}, u32[]{:S(2)}) collective-permute-start(bf16[4,384,161]{1,2,0:T(8,128)(2,1)S(1)} %get-tuple-element.11), channel_id=1, source_target_pairs={{0,4},{4,8},{8,12},{12,16},{16,20},{20,24},{24,28},{28,32},{32,36}... | collective-permute-start | bytes 1483784 | tf_op jit(solution)/shard_map/ppermute | solution.py:17
  119.2 8.2 %collective-permute-done.5 = bf16[4,384,161]{1,2,0:T(8,128)(2,1)S(1)} collective-permute-done((bf16[4,384,161]{1,2,0:T(8,128)(2,1)S(1)}, bf16[4,384,161]{1,2,0:T(8,128)(2,1)S(1)}, u32[]{:S(2)}, u32[]{:S(2)}) %collective-permute-start.5) | collective-permute-done | bytes 494624 | tf_op jit(solution)/shard_map/ppermute | solution.py:20
  128.6 5.0 %collective-permute-done.4 = bf16[4,384,161]{1,2,0:T(8,128)(2,1)S(1)} collective-permute-done((bf16[4,384,161]{1,2,0:T(8,128)(2,1)S(1)}, bf16[4,384,161]{1,2,0:T(8,128)(2,1)S(1)}, u32[]{:S(2)}, u32[]{:S(2)}) %collective-permute-start.4) | collective-permute-done | bytes 494624 | tf_op jit(solution)/shard_map/ppermute | solution.py:17
  135.6 0.3 fusion.241
  136.4 0.3 fusion.243
  137.3 0.3 fusion.245
  138.8 0.4 fusion.50
  139.5 0.4 fusion.74
  139.9 11.5 %all_to_all.22 = bf16[4,2,96,225]{3,2,1,0:T(8,128)(2,1)S(1)} all-to-all(bf16[4,2,96,225]{3,2,1,0:T(8,128)(2,1)S(1)} %stack.21), channel_id=1, replica_groups=mesh['tile'=64,'chan'=4] {'chan'}, dimensions={0} | all-to-all | bytes 691200 | tf_op jit(solution)/shard_map/all_to_all | solution.py:87
  152.4 1.9 %collective-permute-start.7 = (bf16[2,384,161]{1,2,0:T(8,128)(2,1)S(1)}, bf16[2,384,161]{1,2,0:T(8,128)(2,1)S(1)}, u32[]{:S(2)}, u32[]{:S(2)}) collective-permute-start(bf16[2,384,161]{1,2,0:T(8,128)(2,1)S(1)} %get-tuple-element.22), channel_id=1, source_target_pairs={{4,0},{8,4},{12,8},{16,12},{20,16},{24,20},{28,24},{32,28},{36,32}... | collective-permute-start | bytes 741896 | tf_op jit(solution)/shard_map/ppermute | solution.py:20
  154.3 3.9 %collective-permute-start.6 = (bf16[2,384,161]{1,2,0:T(8,128)(2,1)S(1)}, bf16[2,384,161]{1,2,0:T(8,128)(2,1)S(1)}, u32[]{:S(2)}, u32[]{:S(2)}) collective-permute-start(bf16[2,384,161]{1,2,0:T(8,128)(2,1)S(1)} %get-tuple-element.21), channel_id=1, source_target_pairs={{0,4},{4,8},{8,12},{12,16},{16,20},{20,24},{24,28},{28,32},{32,36}... | collective-permute-start | bytes 741896 | tf_op jit(solution)/shard_map/ppermute | solution.py:17
  158.7 3.2 %collective-permute-done.7 = bf16[2,384,161]{1,2,0:T(8,128)(2,1)S(1)} collective-permute-done((bf16[2,384,161]{1,2,0:T(8,128)(2,1)S(1)}, bf16[2,384,161]{1,2,0:T(8,128)(2,1)S(1)}, u32[]{:S(2)}, u32[]{:S(2)}) %collective-permute-start.7) | collective-permute-done | bytes 247328 | tf_op jit(solution)/shard_map/ppermute | solution.py:20
  161.9 6.1 %collective-permute-done.6 = bf16[2,384,161]{1,2,0:T(8,128)(2,1)S(1)} collective-permute-done((bf16[2,384,161]{1,2,0:T(8,128)(2,1)S(1)}, bf16[2,384,161]{1,2,0:T(8,128)(2,1)S(1)}, u32[]{:S(2)}, u32[]{:S(2)}) %collective-permute-start.6) | collective-permute-done | bytes 247328 | tf_op jit(solution)/shard_map/ppermute | solution.py:17
  168.0 0.3 fusion.110
  173.2 0.7 copy.129
  173.9 0.8 copy.130
  174.7 0.8 add_convert_fusion
  (165 shorter events, 24.9 us)
Async XLA Ops:
  0.0 23.3 %copy-start.11 = (bf16[3,3,3,96,16]{3,4,2,1,0:T(8,128)(2,1)S(1)}, bf16[3,3,3,96,16]{3,4,2,1,0:T(8,128)(2,1)}, u32[]{:S(2)}) copy-start(bf16[3,3,3,96,16]{3,4,2,1,0:T(8,128)(2,1)} %param.16) | copy-start | bytes 248836
  1.4 9.9 %all-to-all-start = ((bf16[4,4,4,225]{3,2,1,0:T(4,128)(2,1)}), bf16[4,4,4,225]{3,2,1,0:T(4,128)(2,1)S(1)}, u32[]{:S(2)}, u32[]{:S(2)}) async-start(bf16[4,4,4,225]{3,2,1,0:T(4,128)(2,1)} %stack.18), calls=%async_computation | async-start | bytes 65536 | tf_op jit(solution)/shard_map/all_to_all | solution.py:87
  11.5 9.1 %collective-permute-start.1 = (bf16[4,16,161]{2,1,0:T(8,128)(2,1)S(1)}, bf16[4,16,161]{2,1,0:T(8,128)(2,1)S(1)}, u32[]{:S(2)}, u32[]{:S(2)}) collective-permute-start(bf16[4,16,161]{2,1,0:T(8,128)(2,1)S(1)} %get-tuple-element.27), channel_id=1, source_target_pairs={{4,0},{8,4},{12,8},{16,12},{20,16},{24,20},{28,24},{32,28},{36,32}... | collective-permute-start | bytes 61832 | tf_op jit(solution)/shard_map/ppermute | solution.py:20
  15.8 10.0 %collective-permute-start = (bf16[4,16,161]{2,1,0:T(8,128)(2,1)S(1)}, bf16[4,16,161]{2,1,0:T(8,128)(2,1)S(1)}, u32[]{:S(2)}, u32[]{:S(2)}) collective-permute-start(bf16[4,16,161]{2,1,0:T(8,128)(2,1)S(1)} %get-tuple-element.26), channel_id=1, source_target_pairs={{0,4},{4,8},{8,12},{12,16},{16,20},{20,24},{24,28},{28,32},{32,36}... | collective-permute-start | bytes 61832 | tf_op jit(solution)/shard_map/ppermute | solution.py:17
  29.9 0.7 copy-start.14
  29.9 8.4 %copy-start.15 = (f32[96]{0:T(128)S(1)}, f32[96]{0:T(128)}, u32[]{:S(2)}) copy-start(f32[96]{0:T(128)} %param.19) | copy-start | bytes 1156
  29.9 8.6 %copy-start.12 = (bf16[2,96,225]{2,1,0:T(8,128)(2,1)S(1)}, bf16[2,96,225]{2,1,0:T(8,128)(2,1)}, u32[]{:S(2)}) copy-start(bf16[2,96,225]{2,1,0:T(8,128)(2,1)} %param.18) | copy-start | bytes 259204
  30.8 23.4 %copy-start.3 = (f32[2,225,96]{1,2,0:T(8,128)}, f32[2,225,96]{1,2,0:T(8,128)S(1)}, u32[]{:S(2)}) copy-start(f32[2,225,96]{1,2,0:T(8,128)S(1)} %get-tuple-element.29) | copy-start | bytes 518404
  55.3 9.2 %copy-start.1 = (bf16[3,3,3,96,384]{4,3,2,1,0:T(8,128)(2,1)S(1)}, bf16[3,3,3,96,384]{4,3,2,1,0:T(8,128)(2,1)}, u32[]{:S(2)}) copy-start(bf16[3,3,3,96,384]{4,3,2,1,0:T(8,128)(2,1)} %param.20) | copy-start | bytes 5971972
  55.7 8.8 %copy-start.9 = (bf16[2,4,96,225]{3,2,0,1:T(8,128)(2,1)S(1)}, bf16[2,4,96,225]{3,2,0,1:T(8,128)(2,1)}, u32[]{:S(2)}) copy-start(bf16[2,4,96,225]{3,2,0,1:T(8,128)(2,1)} %get-tuple-element.9) | copy-start | bytes 1036804
  55.7 9.0 %copy-start.7 = (bf16[2,4,96,225]{3,2,0,1:T(8,128)(2,1)S(1)}, bf16[2,4,96,225]{3,2,0,1:T(8,128)(2,1)}, u32[]{:S(2)}) copy-start(bf16[2,4,96,225]{3,2,0,1:T(8,128)(2,1)} %get-tuple-element.10) | copy-start | bytes 1036804
  55.7 9.1 %copy-start.5 = (bf16[2,4,96,225]{3,2,0,1:T(8,128)(2,1)S(1)}, bf16[2,4,96,225]{3,2,0,1:T(8,128)(2,1)}, u32[]{:S(2)}) copy-start(bf16[2,4,96,225]{3,2,0,1:T(8,128)(2,1)} %get-tuple-element.8) | copy-start | bytes 1036804
  55.8 17.3 %collective-permute-start.3 = (bf16[4,384,161]{1,2,0:T(8,128)(2,1)S(1)}, bf16[4,384,161]{1,2,0:T(8,128)(2,1)S(1)}, u32[]{:S(2)}, u32[]{:S(2)}) collective-permute-start(bf16[4,384,161]{1,2,0:T(8,128)(2,1)S(1)} %get-tuple-element.14), channel_id=1, source_target_pairs={{4,0},{8,4},{12,8},{16,12},{20,16},{24,20},{28,24},{32,28},{36,32}... | collective-permute-start | bytes 1483784 | tf_op jit(solution)/shard_map/ppermute | solution.py:20
  62.5 19.0 %collective-permute-start.2 = (bf16[4,384,161]{1,2,0:T(8,128)(2,1)S(1)}, bf16[4,384,161]{1,2,0:T(8,128)(2,1)S(1)}, u32[]{:S(2)}, u32[]{:S(2)}) collective-permute-start(bf16[4,384,161]{1,2,0:T(8,128)(2,1)S(1)} %get-tuple-element.13), channel_id=1, source_target_pairs={{0,4},{4,8},{8,12},{12,16},{16,20},{20,24},{24,28},{28,32},{32,36}... | collective-permute-start | bytes 1483784 | tf_op jit(solution)/shard_map/ppermute | solution.py:17
  86.4 0.7 copy-start.19
  87.1 7.6 %copy-start.16 = (f32[96]{0:T(128)S(1)}, f32[96]{0:T(128)}, u32[]{:S(2)}) copy-start(f32[96]{0:T(128)} %param.23) | copy-start | bytes 1156
  87.1 7.7 %copy-start.13 = (bf16[2,96,225]{2,1,0:T(8,128)(2,1)S(1)}, bf16[2,96,225]{2,1,0:T(8,128)(2,1)}, u32[]{:S(2)}) copy-start(bf16[2,96,225]{2,1,0:T(8,128)(2,1)} %param.22) | copy-start | bytes 259204
  111.8 6.7 %copy-start.2 = (bf16[3,3,3,96,384]{4,3,2,1,0:T(8,128)(2,1)S(1)}, bf16[3,3,3,96,384]{4,3,2,1,0:T(8,128)(2,1)}, u32[]{:S(2)}) copy-start(bf16[3,3,3,96,384]{4,3,2,1,0:T(8,128)(2,1)} %param.24) | copy-start | bytes 5971972
  112.1 6.3 %copy-start.10 = (bf16[2,4,96,225]{3,2,0,1:T(8,128)(2,1)S(1)}, bf16[2,4,96,225]{3,2,0,1:T(8,128)(2,1)}, u32[]{:S(2)}) copy-start(bf16[2,4,96,225]{3,2,0,1:T(8,128)(2,1)} %get-tuple-element.6) | copy-start | bytes 1036804
  112.1 6.6 %copy-start.8 = (bf16[2,4,96,225]{3,2,0,1:T(8,128)(2,1)S(1)}, bf16[2,4,96,225]{3,2,0,1:T(8,128)(2,1)}, u32[]{:S(2)}) copy-start(bf16[2,4,96,225]{3,2,0,1:T(8,128)(2,1)} %get-tuple-element.7) | copy-start | bytes 1036804
  112.1 6.6 %copy-start.6 = (bf16[2,4,96,225]{3,2,0,1:T(8,128)(2,1)S(1)}, bf16[2,4,96,225]{3,2,0,1:T(8,128)(2,1)}, u32[]{:S(2)}) copy-start(bf16[2,4,96,225]{3,2,0,1:T(8,128)(2,1)} %get-tuple-element.5) | copy-start | bytes 1036804
  112.2 15.1 %collective-permute-start.5 = (bf16[4,384,161]{1,2,0:T(8,128)(2,1)S(1)}, bf16[4,384,161]{1,2,0:T(8,128)(2,1)S(1)}, u32[]{:S(2)}, u32[]{:S(2)}) collective-permute-start(bf16[4,384,161]{1,2,0:T(8,128)(2,1)S(1)} %get-tuple-element.12), channel_id=1, source_target_pairs={{4,0},{8,4},{12,8},{16,12},{20,16},{24,20},{28,24},{32,28},{36,32}... | collective-permute-start | bytes 1483784 | tf_op jit(solution)/shard_map/ppermute | solution.py:20
  114.3 19.2 %collective-permute-start.4 = (bf16[4,384,161]{1,2,0:T(8,128)(2,1)S(1)}, bf16[4,384,161]{1,2,0:T(8,128)(2,1)S(1)}, u32[]{:S(2)}, u32[]{:S(2)}) collective-permute-start(bf16[4,384,161]{1,2,0:T(8,128)(2,1)S(1)} %get-tuple-element.11), channel_id=1, source_target_pairs={{0,4},{4,8},{8,12},{12,16},{16,20},{20,24},{24,28},{28,32},{32,36}... | collective-permute-start | bytes 1483784 | tf_op jit(solution)/shard_map/ppermute | solution.py:17
  138.5 0.9 copy-start.4
  138.5 0.9 copy-start.17
  139.8 11.8 %copy-start = (bf16[3,3,48,384]{3,2,1,0:T(8,128)(2,1)S(1)}, bf16[3,3,48,384]{3,2,1,0:T(8,128)(2,1)}, u32[]{:S(2)}) copy-start(bf16[3,3,48,384]{3,2,1,0:T(8,128)(2,1)} %param.26) | copy-start | bytes 995332
  152.4 9.5 %collective-permute-start.7 = (bf16[2,384,161]{1,2,0:T(8,128)(2,1)S(1)}, bf16[2,384,161]{1,2,0:T(8,128)(2,1)S(1)}, u32[]{:S(2)}, u32[]{:S(2)}) collective-permute-start(bf16[2,384,161]{1,2,0:T(8,128)(2,1)S(1)} %get-tuple-element.22), channel_id=1, source_target_pairs={{4,0},{8,4},{12,8},{16,12},{20,16},{24,20},{28,24},{32,28},{36,32}... | collective-permute-start | bytes 741896 | tf_op jit(solution)/shard_map/ppermute | solution.py:20
  154.3 13.7 %collective-permute-start.6 = (bf16[2,384,161]{1,2,0:T(8,128)(2,1)S(1)}, bf16[2,384,161]{1,2,0:T(8,128)(2,1)S(1)}, u32[]{:S(2)}, u32[]{:S(2)}) collective-permute-start(bf16[2,384,161]{1,2,0:T(8,128)(2,1)S(1)} %get-tuple-element.21), channel_id=1, source_target_pairs={{0,4},{4,8},{8,12},{12,16},{16,20},{20,24},{24,28},{28,32},{32,36}... | collective-permute-start | bytes 741896 | tf_op jit(solution)/shard_map/ppermute | solution.py:17
  172.9 1.8 %copy-start.18 = (f32[48]{0:T(128)S(1)}, f32[48]{0:T(128)}, u32[]{:S(2)}) copy-start(f32[48]{0:T(128)} %param.27) | copy-start | bytes 580
